TPU v7x, 32 devices: a whole 2x2x4 slice. The times are simulated.
32 devices in a mesh: pair: 2 (over core), shot: 16 (over z, y, x).
Axes of the slice: x: 2, y: 2, z: 4, core: 2. Of those that a mesh axis runs over, the one named last changes fastest.
Arguments:
- records: bfloat16 [4, 384, 384, 128], P('pair', 'shot'), may hold values from -6 to 6
- surface: float32 [16, 384], P('shot'), may hold values from 0.4 to 1.2
- mirror: int32 [4], replicated, may hold values from 0 to 3, as said below
Outputs:
- predicted: bfloat16 [4, 384, 384, 128], P('pair', 'shot')
Inputs may be any that keep to these rules, and one draw needn't show every extreme that they name: mirror is an involution without fixed points: mirror[mirror[g]] = g and mirror[g] differs from g for every group.
All inputs are finite; a program needn't handle non-finite values.
Results may differ from a plain program's by a relative error of at most 0.0088.
Values may be sent and summed in bfloat16 or wider, within the bound.
A program may use at most 128 MiB of HBM per device.

v0:
```python
import functools
import math

import jax
import jax.numpy as jnp
from jax import lax
from jax.experimental import pallas as pl
from jax.experimental.pallas import tpu as pltpu
from jax.sharding import PartitionSpec as P

ORDERS = 2
MESH = pl.DeviceIdType.MESH


def make_tables(freqs, time):
    row = lax.broadcasted_iota(jnp.int32, (2 * freqs, time), 0)
    product = (row // 2 + 1) * lax.broadcasted_iota(jnp.int32, (2 * freqs, time), 1) % time
    phase = product.astype(jnp.float32) * (2.0 * math.pi / time)
    wave = jnp.where(row % 2 == 0, jnp.cos(phase), -jnp.sin(phase))
    forward = (wave * math.sqrt(2.0 / time)).astype(jnp.bfloat16)
    inverse = (wave / math.sqrt(freqs)).astype(jnp.bfloat16)
    return (forward, inverse)


def kernel(
    chips, cores, mirror_hbm, surface_hbm, forward_ref, records_ref, out_ref,
    traces, stage, send, held, left, block, first, totals, back, surface_ref, mirror_ref,
    small_sems, load_sems, own_sems, send_sems, recv_sems, pass_sems, pass_recv_sems,
    back_send_sems, back_recv_sems,
):
    me = lax.axis_index("shot")
    core = lax.axis_index("pair")
    groups, parts, shots, width = send.shape[1:]
    freqs = parts // 2
    loads = load_sems.shape[1]
    chunk = shots // loads
    half = chips // 2
    quarter = chips // 4
    across = jnp.where(me < half, 0, 1)

    def chip(step):
        return lax.rem(me + step, chips)

    def peer(step):
        return lax.rem(core + step, cores)

    def turned(index, size):
        inner = lax.rem(index + me, size) + size * (index // size)
        return lax.rem(across * size + inner, 2 * size)

    def middle(index):
        return quarter + turned(index, quarter)

    def outer(index):
        place = turned(index, quarter)
        return jnp.where(place < quarter, place, place + half)

    def load(group, index):
        some = pl.ds(index * chunk, chunk)
        return pltpu.make_async_copy(
            records_ref.at[group, some], traces.at[group, some], load_sems.at[group, index]
        )

    for group in range(groups):
        for index in range(loads):
            load(group, index).start()
    surface_copy = pltpu.make_async_copy(surface_hbm, surface_ref, small_sems.at[0])
    mirror_copy = pltpu.make_async_copy(mirror_hbm, mirror_ref, small_sems.at[1])
    surface_copy.start()
    mirror_copy.start()

    barrier = pltpu.get_barrier_semaphore()

    @pl.loop(1, chips)
    def _(step):
        pl.semaphore_signal(barrier, inc=1, device_id=(core, chip(step)), device_id_type=MESH)

    for step in range(1, cores):
        pl.semaphore_signal(barrier, inc=1, device_id=(peer(step), me), device_id_type=MESH)

    def spread(source, target, group):
        return pltpu.make_async_remote_copy(
            src_ref=send.at[target, group],
            dst_ref=held.at[core, group, :, source],
            send_sem=send_sems.at[group, target],
            recv_sem=recv_sems.at[group, source],
            device_id=(core, target),
            device_id_type=MESH,
        )

    def hand_on(source, other, group):
        return pltpu.make_async_remote_copy(
            src_ref=held.at[core, group, :, source],
            dst_ref=held.at[core, group, :, source],
            send_sem=pass_sems.at[other, group, source],
            recv_sem=pass_recv_sems.at[other, group, source],
            device_id=(peer(other), me),
            device_id_type=MESH,
        )

    def keep(group):
        return pltpu.make_async_copy(
            send.at[me, group], held.at[core, group, :, me], own_sems.at[group]
        )

    def send_back(source, target, group):
        return pltpu.make_async_remote_copy(
            src_ref=totals.at[target, group],
            dst_ref=back.at[source, group],
            send_sem=back_send_sems.at[group, target],
            recv_sem=back_recv_sems.at[group, source],
            device_id=(core, target),
            device_id_type=MESH,
        )

    def spread_half(target_of, group):
        @pl.loop(0, half)
        def _(index):
            target = target_of(index)

            @pl.when(target != me)
            def _():
                spread(me, target, group).start()

    for group in range(groups):
        for index in range(loads):
            load(group, index).wait()
            for shot in range(index * chunk, (index + 1) * chunk):
                stage[shot] = lax.dot_general(
                    forward_ref[...], traces[group, shot], (((1,), (1,)), ((), ())),
                    preferred_element_type=jnp.float32,
                )
        for row in range(chips * parts):
            send[row // parts, group, row % parts] = stage[:, row, :].astype(jnp.bfloat16)
        if group == 0:
            pl.semaphore_wait(barrier, chips + cores - 2)
        spread_half(middle, group)
        keep(group).start()
    for group in range(groups):
        spread_half(outer, group)

    surface_copy.wait()
    mirror_copy.wait()
    for group in range(groups):
        keep(group).wait()
        for other in range(1, cores):
            hand_on(me, other, group).start()

        @pl.loop(1, chips)
        def _(step):
            source = chip(step)
            spread(source, source, group).wait_recv()
            for other in range(1, cores):
                hand_on(source, other, group).start()

    @pl.loop(0, chips)
    def _(source):
        for group in range(groups):
            for other in range(1, cores):
                hand_on(source, other, group).wait()

    def matrix(slot, group, part):
        value = held[slot, group, part].astype(jnp.float32)
        return value.reshape(chips * shots, width)

    tall = chips * shots
    span = 16 if chips % 16 == 0 else chips
    tile = width if width % 256 == 0 else 2 * width
    for group in range(groups):
        mate = mirror_ref[core * groups + group]
        mate_slot = mate // groups
        mate_group = lax.rem(mate, groups)
        for freq in range(freqs):
            scale = -surface_ref[pl.ds(freq, 1), :] / math.sqrt(2.0 * width)
            mate_re = matrix(mate_slot, mate_group, 2 * freq)
            mate_im = matrix(mate_slot, mate_group, 2 * freq + 1)
            block[:tall, :width] = mate_re.astype(jnp.bfloat16)
            block[tall:, width:] = mate_re.astype(jnp.bfloat16)
            block[:tall, width:] = mate_im.astype(jnp.bfloat16)
            block[tall:, :width] = (-mate_im).astype(jnp.bfloat16)
            for part in range(2):
                columns = slice(part * width, (part + 1) * width)
                value = matrix(core, group, 2 * freq + part)
                left[:, columns] = (value * scale).astype(jnp.bfloat16)
            for order in range(ORDERS):
                for top in range(0, chips, span):
                    band = slice(top * shots, (top + span) * shots)
                    pieces = []
                    for start in range(0, 2 * width, tile):
                        piece = jnp.dot(
                            left[band, :], block[:, start : start + tile],
                            preferred_element_type=jnp.float32,
                        )
                        if order > 0:
                            piece = piece + first[band, start : start + tile]
                        if order + 1 < ORDERS:
                            first[band, start : start + tile] = piece
                            pieces.append(piece)
                        else:
                            for low in range(start, start + tile, width):
                                total = piece[:, low - start : low - start + width]
                                totals[top : top + span, group, 2 * freq + low // width] = (
                                    total.reshape(span, shots, width).astype(jnp.bfloat16)
                                )
                    if order + 1 < ORDERS:
                        product = jnp.concatenate(pieces, axis=1) if len(pieces) > 1 else pieces[0]
                        wide = jnp.concatenate([scale, scale], axis=1)
                        left[band, :] = (product * wide).astype(jnp.bfloat16)

        @pl.loop(0, chips)
        def _(index):
            target = turned(index, half)

            @pl.when(target != me)
            def _():
                send_back(me, target, group).start()

        for part in range(parts):
            own = totals[me, group, part].astype(jnp.float32)
            back[me, group, part] = own.astype(jnp.bfloat16)

    @pl.loop(1, chips)
    def _(step):
        for group in range(groups):
            spread(me, chip(step), group).wait_send()

    for group in range(groups):

        @pl.loop(0, chips)
        def _(source):
            @pl.when(source != me)
            def _():
                send_back(source, source, group).wait()

            for part in range(parts):
                value = back[source, group, part].astype(jnp.float32)
                stage[:, pl.ds(source * parts + part, 1), :] = value[:, None, :]

        out_ref[group] = stage[...].astype(jnp.bfloat16)


def local(records, surface, mirror):
    chips = lax.axis_size("shot")
    cores = lax.axis_size("pair")
    groups, shots, receivers, time = records.shape
    freqs = surface.shape[0]
    parts = 2 * freqs
    forward, inverse = make_tables(freqs * chips, time)
    tall = chips * shots
    loads = 4 if shots % 4 == 0 else 1
    block_shape = (chips, groups, parts, shots, receivers)
    dma = pltpu.SemaphoreType.DMA
    total_shape = (groups, shots, chips * parts, receivers)
    scratch = [
        (records.shape, jnp.bfloat16),
        ((shots, chips * parts, receivers), jnp.float32),
        (block_shape, jnp.bfloat16),
        ((cores, groups, parts, chips, shots, receivers), jnp.bfloat16),
        ((tall, 2 * receivers), jnp.bfloat16),
        ((2 * tall, 2 * receivers), jnp.bfloat16),
        ((tall, 2 * receivers), jnp.float32),
        (block_shape, jnp.bfloat16),
        (block_shape, jnp.bfloat16),
    ]
    held_bytes = sum(math.prod(shape) * jnp.dtype(kind).itemsize for shape, kind in scratch)
    roomy = held_bytes < 24 * 1024 * 1024
    grant = held_bytes + 8 * 1024 * 1024 if roomy else 67043328
    out_shape = pltpu.VMEM if roomy else jax.ShapeDtypeStruct
    total = pl.pallas_call(
        functools.partial(kernel, chips, cores),
        out_shape=out_shape(total_shape, jnp.bfloat16),
        in_specs=[
            pl.BlockSpec(memory_space=pltpu.HBM),
            pl.BlockSpec(memory_space=pltpu.HBM),
            pl.BlockSpec(memory_space=pltpu.VMEM),
            pl.BlockSpec(memory_space=pltpu.HBM),
        ],
        out_specs=pl.BlockSpec(memory_space=pltpu.VMEM),
        scratch_shapes=[
            *(pltpu.VMEM(shape, kind) for shape, kind in scratch),
            pltpu.VMEM(surface.shape, jnp.float32),
            pltpu.SMEM(mirror.shape, jnp.int32),
            dma((2,)),
            dma((groups, loads)),
            dma((groups,)),
            dma((groups, chips)),
            dma((groups, chips)),
            dma((cores, groups, chips)),
            dma((cores, groups, chips)),
            dma((groups, chips)),
            dma((groups, chips)),
        ],
        compiler_params=pltpu.CompilerParams(
            collective_id=0, has_side_effects=True, vmem_limit_bytes=grant
        ),
    )(
        pltpu.with_memory_space_constraint(mirror, pltpu.HBM),
        pltpu.with_memory_space_constraint(surface, pltpu.HBM),
        forward,
        pltpu.with_memory_space_constraint(records, pltpu.HBM),
    )
    return jnp.einsum("gskr,kt->gsrt", total, inverse, preferred_element_type=jnp.float32).astype(
        jnp.bfloat16
    )


def solution(mesh):
    return jax.shard_map(
        local,
        mesh=mesh,
        in_specs=(P("pair", "shot", None, None), P("shot", None), P()),
        out_specs=P("pair", "shot", None, None),
        check_vma=False,
    )
```

profile of v0, /device:TPU:12, one launch (start us, length us, event | category | flops | bytes accessed | tf_op | source)
XLA Modules:
  0.0 63.9 jit_solution(8475660496860334424)
XLA Ops:
  0.0 0.2 multiply_convert_fusion.1.forward_ref
  0.2 60.4 %shard_map.37 = bf16[2,24,32,384]{3,2,1,0:T(8,128)(2,1)S(1)} custom-call(s32[4]{0:T(128)} %mirror_hbm.1, f32[1,384]{1,0:T(1,128)} %surface_hbm.1, bf16[32,128]{1,0:T(8,128)(2,1)S(1)} %multiply_convert_fusion.1.forward_ref, bf16[2,24,384,128]{3,2,1,0:T(8,128)(2,1)} %records_ref.1), custom_call_target="tpu_custom_call" | custom-call | tf_op jit(solution)/shard_map/pallas_call | solution.py:269
  60.6 3.3 %convolution_convert_fusion = bf16[2,24,384,128]{3,2,1,0:T(8,128)(2,1)} fusion(bf16[2,24,32,384]{3,2,1,0:T(8,128)(2,1)S(1)} %shard_map.37, s32[32]{0:T(128)S(1)} %get-tuple-element.7, s32[32]{0:T(128)S(1)} %get-tuple-element.9, s32[32]{0:T(128)S(1)} %get-tuple-element.8, s32[32]{0:T(128)S(1)} %get-tuple-element.10, pred[32]{0:T(512)(128)(4,1)S(1)} %get-tuple-element.5, ...), kind=kOutput, calls=%fused_computation | convolution fusion | flops 153444352 | bytes 5898816 | tf_op jit(solution)/shard_map/gskr,kt->gsrt/dot_general | solution.py:302
  (3 shorter events, 0.0 us)
where the time goes:
time: 64.4 us; the launch traced here: 63.9 us
  Pallas kernels  60.4 us (94%)
  matrix products  3.31 us (5%)
    pallas_call x1, Pallas kernels, local(): pl.pallas_call(functools.partial(kernel, chips, cores), out_shape=out_sha...  60.4 us
    dot_general x1, matrix products, local(): jnp.einsum('gskr,kt->gsrt', total, inverse, preferred_element_type=jnp.fl...  3.31 us

commit v1 on v0

v1 whole, which is shorter than its diff:
```python
import functools
import math

import jax
import jax.numpy as jnp
from jax import lax
from jax.experimental import pallas as pl
from jax.experimental.pallas import tpu as pltpu
from jax.sharding import PartitionSpec as P

ORDERS = 2
MESH = pl.DeviceIdType.MESH
VMEM_BYTES = 67043328
LANES = 128


def make_tables(freqs, time):
    row = lax.broadcasted_iota(jnp.int32, (2 * freqs, time), 0)
    product = (row // 2 + 1) * lax.broadcasted_iota(jnp.int32, (2 * freqs, time), 1) % time
    phase = product.astype(jnp.float32) * (2.0 * math.pi / time)
    wave = jnp.where(row % 2 == 0, jnp.cos(phase), -jnp.sin(phase))
    forward = (wave * math.sqrt(2.0 / time)).astype(jnp.bfloat16)
    inverse = (wave / math.sqrt(freqs)).astype(jnp.bfloat16)
    return (forward, inverse)


def kernel(chips, cores, lanes, stages, mirror_hbm, surface_hbm, forward_ref, inverse_ref, records_ref, out_ref, *scratch):
    held = scratch[:lanes]
    stage = scratch[lanes : lanes + stages]
    (
        send, left, block, first, totals, back, surface_ref, mirror_ref,
        small_sems, load_sems, own_sems, send_sems, recv_sems, lane_sems, lane_recv_sems,
        pass_sems, pass_recv_sems, back_own_sems, back_send_sems, back_recv_sems, surface_sems,
    ) = scratch[lanes + stages :]
    me = lax.axis_index("shot")
    core = lax.axis_index("pair")
    _, groups, parts, shots, width = send.shape
    freqs = parts // 2
    columns = chips // lanes
    half = columns // 2
    rows = chips * parts
    strips = width // LANES
    loads = load_sems.shape[1]
    chunk = shots // loads
    lane = lax.rem(me, lanes)
    column = me // lanes
    side = column // half

    def lanes_of(strip):
        return slice(strip * LANES, (strip + 1) * LANES)

    def chip(there):
        return there * lanes + lane

    def beside(step):
        return column * lanes + lax.rem(lane + step, lanes)

    def peer(step):
        return lax.rem(core + step, cores)

    def away(index):
        return (1 - side) * half + lax.rem(index + column, half)

    def away_in_order(index):
        return (1 - side) * half + index

    def near(index):
        return side * half + lax.rem(index + column, half)

    def load(group, index):
        some = pl.ds(index * chunk, chunk)
        return pltpu.make_async_copy(
            records_ref.at[group, some], out_ref.at[group, some], load_sems.at[group, index]
        )

    for group in range(groups):
        for index in range(loads):
            load(group, index).start()
    surface_copy = pltpu.make_async_copy(surface_hbm, surface_ref.at[lane], small_sems.at[0])
    mirror_copy = pltpu.make_async_copy(mirror_hbm, mirror_ref, small_sems.at[1])
    surface_copy.start()
    mirror_copy.start()

    barrier = pltpu.get_barrier_semaphore()

    @pl.loop(1, columns)
    def _(step):
        there = lax.rem(column + step, columns)
        pl.semaphore_signal(barrier, inc=1, device_id=(core, chip(there)), device_id_type=MESH)

    for step in range(1, lanes):
        pl.semaphore_signal(barrier, inc=1, device_id=(core, beside(step)), device_id_type=MESH)
    for step in range(1, cores):
        pl.semaphore_signal(barrier, inc=1, device_id=(peer(step), me), device_id_type=MESH)

    def spread(phase, group, source, target):
        return pltpu.make_async_remote_copy(
            src_ref=send.at[target * lanes + phase, group],
            dst_ref=held[phase].at[core, group, :, source, lane],
            send_sem=send_sems.at[phase, group, target],
            recv_sem=recv_sems.at[phase, group, source],
            device_id=(core, chip(target)),
            device_id_type=MESH,
        )

    def keep(phase, group):
        return pltpu.make_async_copy(
            send.at[column * lanes + phase, group],
            held[phase].at[core, group, :, column, lane],
            own_sems.at[phase, group],
        )

    def lane_on(phase, group, source, source_lane, step):
        return pltpu.make_async_remote_copy(
            src_ref=held[phase].at[core, group, :, source, source_lane],
            dst_ref=held[phase].at[core, group, :, source, source_lane],
            send_sem=lane_sems.at[phase, group, step, source],
            recv_sem=lane_recv_sems.at[phase, group, step, source],
            device_id=(core, beside(step)),
            device_id_type=MESH,
        )

    def hand_on(phase, group, source, source_lane, other):
        return pltpu.make_async_remote_copy(
            src_ref=held[phase].at[core, group, :, source, source_lane],
            dst_ref=held[phase].at[core, group, :, source, source_lane],
            send_sem=pass_sems.at[phase, group, other - 1, source, source_lane],
            recv_sem=pass_recv_sems.at[phase, group, other - 1, source, source_lane],
            device_id=(peer(other), me),
            device_id_type=MESH,
        )

    def pass_on(phase, group, source, source_lane):
        for other in range(1, cores):
            hand_on(phase, group, source, source_lane, other).start()

    def send_back(phase, group, source, target):
        return pltpu.make_async_remote_copy(
            src_ref=totals.at[phase, target, group],
            dst_ref=back.at[source * lanes + phase, group],
            send_sem=back_send_sems.at[phase, group, target],
            recv_sem=back_recv_sems.at[phase, group, source],
            device_id=(core, chip(target)),
            device_id_type=MESH,
        )

    def keep_back(phase, group):
        return pltpu.make_async_copy(
            totals.at[phase, column, group],
            back.at[column * lanes + phase, group],
            back_own_sems.at[phase, group],
        )

    def to_all(start, away=away):
        @pl.loop(0, half)
        def _(index):
            start(away(index))

        @pl.loop(1, half)
        def _(index):
            start(near(index))

    def spectra(group):
        for index in range(loads):
            load(group, index).wait()
            for shot in range(index * chunk, (index + 1) * chunk):
                value = lax.dot_general(
                    forward_ref[...], out_ref[group, shot], (((1,), (1,)), ((), ())),
                    preferred_element_type=jnp.float32,
                )
                for strip in range(strips):
                    stage[0][strip, shot * rows : (shot + 1) * rows] = value[:, lanes_of(strip)]
        for row in range(rows):
            for strip in range(strips):
                send[row // parts, group, row % parts, :, lanes_of(strip)] = (
                    stage[0][strip, pl.ds(row, shots, stride=rows), :].astype(jnp.bfloat16)
                )

    def spread_all(phase, group):
        to_all(lambda target: spread(phase, group, column, target).start())
        keep(phase, group).start()

    def relay(phase, group):
        def step_on(source):
            for step in range(1, lanes):
                lane_on(phase, group, source, lane, step).start()
            pass_on(phase, group, source, lane)

        keep(phase, group).wait()
        step_on(column)

        @pl.loop(1, half)
        def _(index):
            source = near(index)
            spread(phase, group, source, source).wait_recv()
            step_on(source)

        @pl.loop(0, half)
        def _(index):
            source = away(index)
            spread(phase, group, source, source).wait_recv()
            step_on(source)

        if lanes > 1:
            @pl.loop(0, columns)
            def _(index):
                source = lax.rem(column + index, columns)
                for step in range(1, lanes):
                    source_lane = lax.rem(lane + lanes - step, lanes)
                    lane_on(phase, group, source, source_lane, step).wait_recv()
                    pass_on(phase, group, source, source_lane)

    def settle(phase):
        @pl.loop(0, columns)
        def _(source):
            for group in range(groups):
                for source_lane in range(lanes):
                    for other in range(1, cores):
                        hand_on(phase, group, source, source_lane, other).wait_recv()

    def matrix(value):
        value = value.astype(jnp.float32)
        return value.reshape(-1, width)

    tall = chips * shots
    tile = width if width % 256 == 0 else 2 * width

    def predict(phase, group):
        mate = mirror_ref[core * groups + group]
        mate_slot = mate // groups
        mate_group = lax.rem(mate, groups)
        for freq in range(freqs):
            scale = -surface_ref[phase, pl.ds(freq, 1), :] / math.sqrt(2.0 * width)
            mate_re = matrix(held[phase][mate_slot, mate_group, 2 * freq])
            mate_im = matrix(held[phase][mate_slot, mate_group, 2 * freq + 1])
            block[:tall, :width] = mate_re.astype(jnp.bfloat16)
            block[tall:, width:] = mate_re.astype(jnp.bfloat16)
            block[:tall, width:] = mate_im.astype(jnp.bfloat16)
            block[tall:, :width] = (-mate_im).astype(jnp.bfloat16)
            for part in range(2):
                value = matrix(held[phase][core, group, 2 * freq + part, :, lane])
                left[:, part * width : (part + 1) * width] = (value * scale).astype(jnp.bfloat16)
            span = 16 if columns % 16 == 0 else columns
            for order in range(ORDERS):
                for top in range(0, columns, span):
                    band = slice(top * shots, (top + span) * shots)
                    pieces = []
                    for start in range(0, 2 * width, tile):
                        piece = jnp.dot(
                            left[band, :], block[:, start : start + tile],
                            preferred_element_type=jnp.float32,
                        )
                        if order > 0:
                            piece = piece + first[band, start : start + tile]
                        if order + 1 < ORDERS:
                            first[band, start : start + tile] = piece
                            pieces.append(piece)
                        else:
                            for low in range(start, start + tile, width):
                                total = piece[:, low - start : low - start + width]
                                totals[phase, top : top + span, group, 2 * freq + low // width] = (
                                    total.reshape(span, shots, width).astype(jnp.bfloat16)
                                )
                    if order + 1 < ORDERS:
                        product = jnp.concatenate(pieces, axis=1) if len(pieces) > 1 else pieces[0]
                        wide = jnp.concatenate([scale, scale], axis=1)
                        left[band, :] = (product * wide).astype(jnp.bfloat16)
        last = phase + 1 == lanes and group + 1 == groups
        to_all(
            lambda target: send_back(phase, group, column, target).start(),
            away_in_order if last else away,
        )
        keep_back(phase, group).start()

    def collect(phase, group):
        here = stage[group % stages]

        def unpack(source):
            place = source * lanes + phase
            for part in range(parts):
                value = back[place, group, part].astype(jnp.float32)
                for strip in range(strips):
                    here[strip, pl.ds(place * parts + part, shots, stride=rows), :] = (
                        value[:, lanes_of(strip)]
                    )

        keep_back(phase, group).wait()
        unpack(column)

        @pl.loop(1, half)
        def _(index):
            source = near(index)
            send_back(phase, group, source, source).wait_recv()
            unpack(source)

        @pl.loop(0, half)
        def _(index):
            source = away(index)
            send_back(phase, group, source, source).wait_recv()
            unpack(source)

    def invert(group):
        here = stage[group % stages]
        for shot in range(shots):
            for strip in range(strips):
                value = here[strip, shot * rows : (shot + 1) * rows].astype(jnp.bfloat16)
                out_ref[group, shot, lanes_of(strip), :] = lax.dot_general(
                    value, inverse_ref[...], (((0,), (0,)), ((), ())),
                    preferred_element_type=jnp.float32,
                ).astype(jnp.bfloat16)

    def surface_on(step, source_lane):
        return pltpu.make_async_remote_copy(
            src_ref=surface_ref.at[source_lane],
            dst_ref=surface_ref.at[source_lane],
            send_sem=surface_sems.at[0, step],
            recv_sem=surface_sems.at[1, step],
            device_id=(core, beside(step)),
            device_id_type=MESH,
        )

    for group in range(groups):
        spectra(group)
        if group == 0:
            pl.semaphore_wait(barrier, columns + lanes + cores - 3)
        spread_all(0, group)
    for phase in range(1, lanes):
        for group in range(groups):
            spread_all(phase, group)

    surface_copy.wait()
    mirror_copy.wait()
    for step in range(1, lanes):
        surface_on(step, lane).start()
    for group in range(groups):
        relay(0, group)
    for step in range(1, lanes):
        surface_on(step, lax.rem(lane + lanes - step, lanes)).wait_recv()
    settle(0)
    for phase in range(lanes):
        for group in range(groups):
            predict(phase, group)
            if phase + 1 < lanes:
                relay(phase + 1, group)
        if phase + 1 < lanes:
            settle(phase + 1)

    for step in range(1, lanes):
        surface_on(step, lane).wait_send()

    @pl.loop(0, columns)
    def _(source):
        for phase in range(lanes):
            for group in range(groups):
                for step in range(1, lanes):
                    lane_on(phase, group, source, lane, step).wait_send()
                for source_lane in range(lanes):
                    for other in range(1, cores):
                        hand_on(phase, group, source, source_lane, other).wait_send()

                @pl.when(source != column)
                def _():
                    spread(phase, group, column, source).wait_send()

    for phase in range(lanes - 1):
        for group in range(groups):
            collect(phase, group)
    for group in range(groups):
        collect(lanes - 1, group)
        invert(group)

    @pl.loop(0, columns)
    def _(target):
        @pl.when(target != column)
        def _():
            for phase in range(lanes):
                for group in range(groups):
                    send_back(phase, group, column, target).wait_send()


def local(records, surface, mirror):
    chips = lax.axis_size("shot")
    cores = lax.axis_size("pair")
    groups, shots, receivers, time = records.shape
    freqs = surface.shape[0]
    parts = 2 * freqs
    forward, inverse = make_tables(freqs * chips, time)
    loads = 4 if shots % 4 == 0 else 1
    dma = pltpu.SemaphoreType.DMA

    def buffers(lanes, stages):
        columns = chips // lanes
        tall = columns * shots
        held = ((cores, groups, parts, columns, lanes, shots, receivers), jnp.bfloat16)
        stage = ((receivers // LANES, shots * chips * parts, LANES), jnp.float32)
        return [held] * lanes + [stage] * stages + [
            ((chips, groups, parts, shots, receivers), jnp.bfloat16),
            ((tall, 2 * receivers), jnp.bfloat16),
            ((2 * chips * shots, 2 * receivers), jnp.bfloat16),
            ((tall, 2 * receivers), jnp.float32),
            ((lanes, columns, groups, parts, shots, receivers), jnp.bfloat16),
            ((chips, groups, parts, shots, receivers), jnp.bfloat16),
            ((lanes, freqs, receivers), jnp.float32),
        ]

    def size(shapes):
        return sum(math.prod(shape) * jnp.dtype(kind).itemsize for shape, kind in shapes)

    lanes, stages = 2, groups
    scratch = buffers(lanes, stages)
    out_bytes = records.size * records.dtype.itemsize
    roomy = chips % 4 == 0 and out_bytes + size(scratch) < 40 * 1024 * 1024
    if not roomy:
        lanes, stages = 1, 1
        scratch = buffers(lanes, stages)
    columns = chips // lanes
    grant = min(size(scratch) + 8 * 1024 * 1024, VMEM_BYTES) if roomy else VMEM_BYTES
    out_shape = pltpu.VMEM if roomy else jax.ShapeDtypeStruct
    each = (lanes, groups)
    return pl.pallas_call(
        functools.partial(kernel, chips, cores, lanes, stages),
        out_shape=out_shape(records.shape, jnp.bfloat16),
        in_specs=[
            pl.BlockSpec(memory_space=pltpu.HBM),
            pl.BlockSpec(memory_space=pltpu.HBM),
            pl.BlockSpec(memory_space=pltpu.VMEM),
            pl.BlockSpec(memory_space=pltpu.VMEM),
            pl.BlockSpec(memory_space=pltpu.HBM),
        ],
        out_specs=pl.BlockSpec(memory_space=pltpu.VMEM),
        scratch_shapes=[
            *(pltpu.VMEM(shape, kind) for shape, kind in scratch),
            pltpu.SMEM(mirror.shape, jnp.int32),
            dma((2,)),
            dma((groups, loads)),
            dma(each),
            dma((*each, columns)),
            dma((*each, columns)),
            dma((*each, lanes, columns)),
            dma((*each, lanes, columns)),
            dma((*each, cores - 1, columns, lanes)),
            dma((*each, cores - 1, columns, lanes)),
            dma(each),
            dma((*each, columns)),
            dma((*each, columns)),
            dma((2, lanes)),
        ],
        compiler_params=pltpu.CompilerParams(
            collective_id=0, has_side_effects=True, vmem_limit_bytes=grant
        ),
    )(
        pltpu.with_memory_space_constraint(mirror, pltpu.HBM),
        pltpu.with_memory_space_constraint(surface, pltpu.HBM),
        forward,
        inverse,
        pltpu.with_memory_space_constraint(records, pltpu.HBM),
    )


def solution(mesh):
    return jax.shard_map(
        local,
        mesh=mesh,
        in_specs=(P("pair", "shot", None, None), P("shot", None), P()),
        out_specs=P("pair", "shot", None, None),
        check_vma=False,
    )
```

time: 64.4 us -> 71.6 us (1.11)
  Pallas kernels: 60.4 us -> 69.1 us
  matrix products: 3.31 us -> 0 us
  local copies, waits for them, and re-layouts: 0 us -> 2.19 us
    pallas_call x1, Pallas kernels: 60.4 us -> 69.1 us  [local(): pl.pallas_call(functools.partial(kernel, chips, cores, lanes, stages), ou...]
    dot_general x1 -> x0, matrix products: 3.31 us -> none  [local(): jnp.einsum('gskr,kt->gsrt', total, inverse, preferred_element_type=jnp.fl...]
    unnamed x0 -> x1, local copies, waits for them, and re-layouts: none -> 2.19 us
where the time goes in v1:
time: 71.6 us; the launch traced here: 71.5 us
  Pallas kernels  69.1 us (97%)
  local copies, waits for them, and re-layouts  2.19 us (3%)
    pallas_call x1, Pallas kernels, local(): pl.pallas_call(functools.partial(kernel, chips, cores, lanes, stages), ou...  69.1 us
    unnamed x1, local copies, waits for them, and re-layouts  2.19 us

profile of v1, /device:TPU:12, one launch (start us, length us, event | category | flops | bytes accessed | tf_op | source)
XLA Modules:
  0.0 71.5 jit_solution(15663889105773033825)
XLA Ops:
  0.0 0.2 multiply_convert_fusion
  0.2 69.1 %shard_map.37 = bf16[2,24,384,128]{3,2,1,0:T(8,128)(2,1)S(1)} custom-call(s32[4]{0:T(128)} %mirror_hbm.1, f32[1,384]{1,0:T(1,128)} %surface_hbm.1, bf16[32,128]{1,0:T(8,128)(2,1)S(1)} %get-tuple-element.6.forward_ref, bf16[32,128]{1,0:T(8,128)(2,1)S(1)} %get-tuple-element.5.inverse_ref, bf16[2,24,384,128]{3,2,1,0:T(8,128)(2,1)} %records_ref.1), custom_call_target="tpu_custom_call" | custom-call | tf_op jit(solution)/shard_map/pallas_call | solution.py:420
  69.3 2.2 %copy.5 = bf16[2,24,384,128]{3,2,1,0:T(8,128)(2,1)} copy(bf16[2,24,384,128]{3,2,1,0:T(8,128)(2,1)S(1)} %shard_map.37) | data formatting | bytes 9437184
  (3 shorter events, 0.0 us)

commit v2 on v0

v2 whole, which is shorter than its diff:
```python
import functools
import math

import jax
import jax.numpy as jnp
import numpy as np
from jax import lax
from jax.experimental import pallas as pl
from jax.experimental.pallas import tpu as pltpu
from jax.sharding import PartitionSpec as P

ORDERS = 2
MESH = pl.DeviceIdType.MESH
VMEM_BYTES = 67043328
LANES = 128


def make_tables(freqs, time):
    row = np.arange(2 * freqs)[:, None]
    product = (row // 2 + 1) * np.arange(time)[None, :] % time
    phase = product.astype(np.float32) * np.float32(2.0 * math.pi / time)
    wave = np.where(row % 2 == 0, np.cos(phase), -np.sin(phase))
    forward = (wave * math.sqrt(2.0 / time)).astype(jnp.bfloat16)
    inverse = (wave / math.sqrt(freqs)).astype(jnp.bfloat16)
    return np.stack([forward, inverse])


def cut(shots, group, groups):
    whole = ((0, shots),)
    if shots % 8 or shots < 16:
        return whole, whole
    first = ((0, 8), (8, shots - 8)) if group == 0 else whole
    last = ((0, shots - 8), (shots - 8, 8)) if group + 1 == groups else whole
    return first, last


def kernel(
    chips, cores, mirror_hbm, surface_hbm, tables_hbm, records_ref, out_ref,
    traces, stage, send, held, left, block, first, totals, back, surface_ref, tables, mirror_ref,
    small_sems, load_sems, own_sems, send_sem, recv_sems, pass_sems, back_send_sem, back_recv_sems, out_sem,
    entered,
):
    me = lax.axis_index("shot")
    core = lax.axis_index("pair")
    groups, parts, shots, width = send.shape[1:]
    freqs = parts // 2
    rows = chips * parts
    strips = width // LANES
    half = chips // 2
    quarter = chips // 4
    across = jnp.where(me < half, 0, 1)
    plane = me // quarter
    planes = (plane, plane + 1 - 2 * lax.rem(plane, 2), 3 * (1 - across), 2 - across)
    cuts = [cut(shots, group, groups) for group in range(groups)]

    def strip_of(strip):
        return slice(strip * LANES, (strip + 1) * LANES)

    def level(step):
        return plane * quarter + lax.rem(me + step, quarter)

    def upright(there):
        return there * quarter + lax.rem(me, quarter)

    def peer(step):
        return lax.rem(core + step, cores)

    def turned(index, size):
        inner = lax.rem(index + me, size) + size * (index // size)
        return lax.rem(across * size + inner, 2 * size)

    def middle(index):
        return quarter + turned(index, quarter)

    def outer(index):
        place = turned(index, quarter)
        return jnp.where(place < quarter, place, place + half)

    def load(group, index):
        some = pl.ds(*cuts[group][0][index])
        return pltpu.make_async_copy(
            records_ref.at[group, some], traces.at[group, some], load_sems.at[group, index]
        )

    for group in range(groups):
        for index in range(len(cuts[group][0])):
            load(group, index).start()
    surface_copy = pltpu.make_async_copy(surface_hbm, surface_ref, small_sems.at[0])
    mirror_copy = pltpu.make_async_copy(mirror_hbm, mirror_ref, small_sems.at[1])
    tables_copy = pltpu.make_async_copy(tables_hbm, tables, small_sems.at[2])
    tables_copy.start()
    surface_copy.start()
    mirror_copy.start()

    barrier = pltpu.get_barrier_semaphore()

    @pl.loop(1, quarter)
    def _(step):
        pl.semaphore_signal(barrier, inc=1, device_id=(core, level(step)), device_id_type=MESH)

    for step in range(1, 4):
        pl.semaphore_signal(barrier, inc=1, device_id=(core, upright(planes[step])), device_id_type=MESH)
    for step in range(1, cores):
        pl.semaphore_signal(barrier, inc=1, device_id=(peer(step), me), device_id_type=MESH)

    def spread(source, target, group, some):
        return pltpu.make_async_remote_copy(
            src_ref=send.at[target, group, :, some],
            dst_ref=held.at[core, group, :, source, some],
            send_sem=send_sem,
            recv_sem=recv_sems.at[group, source // quarter],
            device_id=(core, target),
            device_id_type=MESH,
        )

    def arrived(group, there, count):
        some = held.at[core, group, :, pl.ds(0, count)]
        return pltpu.make_async_remote_copy(
            src_ref=some,
            dst_ref=some,
            send_sem=send_sem,
            recv_sem=recv_sems.at[group, there],
            device_id=(core, me),
            device_id_type=MESH,
        )

    def hand_on(some, other):
        return pltpu.make_async_remote_copy(
            src_ref=some,
            dst_ref=some,
            send_sem=pass_sems.at[other - 1, 0],
            recv_sem=pass_sems.at[other - 1, 1],
            device_id=(peer(other), me),
            device_id_type=MESH,
        )

    def keep(group):
        return pltpu.make_async_copy(
            send.at[me, group], held.at[core, group, :, me], own_sems.at[group]
        )

    def send_back(source, target, group, index):
        some = pl.ds(*cuts[group][1][index])
        return pltpu.make_async_remote_copy(
            src_ref=totals.at[target, group, :, some],
            dst_ref=back.at[source, group, :, some],
            send_sem=back_send_sem,
            recv_sem=back_recv_sems.at[group, index, source // quarter],
            device_id=(core, target),
            device_id_type=MESH,
        )

    def returned(group, index, there, count):
        some = back.at[pl.ds(0, count), group, :, pl.ds(*cuts[group][1][index])]
        return pltpu.make_async_remote_copy(
            src_ref=some,
            dst_ref=some,
            send_sem=back_send_sem,
            recv_sem=back_recv_sems.at[group, index, there],
            device_id=(core, me),
            device_id_type=MESH,
        )

    def sent(buffer, sem):
        some = buffer.at[pl.ds(0, chips - 1)]
        return pltpu.make_async_remote_copy(
            src_ref=some,
            dst_ref=some,
            send_sem=sem,
            recv_sem=recv_sems.at[0, 0],
            device_id=(core, me),
            device_id_type=MESH,
        )

    def give(group, index):
        some = pl.ds(*cuts[group][1][index])
        return pltpu.make_async_copy(
            traces.at[group, some], out_ref.at[group, some], out_sem
        )

    def spread_half(target_of, group):
        @pl.loop(0, half)
        def _(step):
            target = target_of(step)

            @pl.when(lax.rem(target, quarter) != lax.rem(me, quarter) if group == 0 else target != me)
            def _():
                spread(me, target, group, pl.ds(0, shots)).start()

    def spectra(group, index):
        start, size = cuts[group][0][index]
        load(group, index).wait()
        for shot in range(start, start + size):
            value = lax.dot_general(
                tables[0], traces[group, shot], (((1,), (1,)), ((), ())),
                preferred_element_type=jnp.float32,
            )
            for strip in range(strips):
                stage[strip, shot * rows : (shot + 1) * rows] = value[:, strip_of(strip)]
        for row in range(rows):
            for strip in range(strips):
                value = stage[strip, pl.ds(start * rows + row, size, stride=rows), :]
                send[row // parts, group, row % parts, start : start + size, strip_of(strip)] = (
                    value.astype(jnp.bfloat16)
                )

    tables_copy.wait()
    for index in range(len(cuts[0][0])):
        spectra(0, index)
        if index == 0:
            pl.semaphore_wait(barrier, quarter + 2 + cores - 1)

            @pl.loop(1, quarter)
            def _(step):
                pl.semaphore_signal(entered, inc=1, device_id=(core, level(step)), device_id_type=MESH)

        for order in (3, 2, 1):
            spread(me, upright(planes[order]), 0, pl.ds(*cuts[0][0][index])).start()
    keep(0).start()
    pl.semaphore_wait(entered, quarter - 1)
    spread_half(middle, 0)
    for group in range(1, groups):
        for index in range(len(cuts[group][0])):
            spectra(group, index)
        spread_half(middle, group)
        keep(group).start()
    for group in range(groups):
        spread_half(outer, group)

    surface_copy.wait()
    mirror_copy.wait()
    for group in range(groups):
        for order, there in enumerate(planes):
            if order == 0:
                keep(group).wait()
            arrived(group, there, quarter - 1 if order == 0 else quarter).wait_recv()
            for other in range(1, cores):
                hand_on(held.at[core, group, :, pl.ds(there * quarter, quarter)], other).start()
    for other in range(1, cores):
        hand_on(held.at[core], other).wait()

    def matrix(slot, group, part):
        value = held[slot, group, part].astype(jnp.float32)
        return value.reshape(chips * shots, width)

    tall = chips * shots
    span = 16 if chips % 16 == 0 else chips
    tile = width if width % 256 == 0 else 2 * width
    for group in range(groups):
        mate = mirror_ref[core * groups + group]
        mate_slot = mate // groups
        mate_group = lax.rem(mate, groups)
        for freq in range(freqs):
            scale = -surface_ref[pl.ds(freq, 1), :] / math.sqrt(2.0 * width)
            mate_re = matrix(mate_slot, mate_group, 2 * freq)
            mate_im = matrix(mate_slot, mate_group, 2 * freq + 1)
            block[:tall, :width] = mate_re.astype(jnp.bfloat16)
            block[tall:, width:] = mate_re.astype(jnp.bfloat16)
            block[:tall, width:] = mate_im.astype(jnp.bfloat16)
            block[tall:, :width] = (-mate_im).astype(jnp.bfloat16)
            for part in range(2):
                columns = slice(part * width, (part + 1) * width)
                value = matrix(core, group, 2 * freq + part)
                left[:, columns] = (value * scale).astype(jnp.bfloat16)
            for order in range(ORDERS):
                for top in range(0, chips, span):
                    band = slice(top * shots, (top + span) * shots)
                    pieces = []
                    for start in range(0, 2 * width, tile):
                        piece = jnp.dot(
                            left[band, :], block[:, start : start + tile],
                            preferred_element_type=jnp.float32,
                        )
                        if order > 0:
                            piece = piece + first[band, start : start + tile]
                        if order + 1 < ORDERS:
                            first[band, start : start + tile] = piece
                            pieces.append(piece)
                        else:
                            for low in range(start, start + tile, width):
                                total = piece[:, low - start : low - start + width]
                                totals[top : top + span, group, 2 * freq + low // width] = (
                                    total.reshape(span, shots, width).astype(jnp.bfloat16)
                                )
                    if order + 1 < ORDERS:
                        product = jnp.concatenate(pieces, axis=1) if len(pieces) > 1 else pieces[0]
                        wide = jnp.concatenate([scale, scale], axis=1)
                        left[band, :] = (product * wide).astype(jnp.bfloat16)

        last = group + 1 == groups
        pieces = range(len(cuts[group][1]))
        if last:
            for index in pieces:
                send_back(me, (1 - across) * half, group, index).start()
        for index in pieces:

            @pl.loop(1 if last else 0, chips)
            def _(step):
                target = lax.rem((1 - across) * half + step, chips) if last else turned(step, half)

                @pl.when(target != me)
                def _():
                    send_back(me, target, group, index).start()

    sent(send, send_sem).wait_send()

    for group in range(groups):
        for index, (start, size) in enumerate(cuts[group][1]):

            def unpack(buffer, source):
                for part in range(parts):
                    value = buffer[source, group, part, start : start + size].astype(jnp.float32)
                    place = start * rows + source * parts + part
                    for strip in range(strips):
                        stage[strip, pl.ds(place, size, stride=rows), :] = value[:, strip_of(strip)]

            unpack(totals, me)
            for order, there in enumerate(planes):
                returned(group, index, there, quarter - 1 if order == 0 else quarter).wait_recv()

                @pl.loop(1 if order == 0 else 0, quarter)
                def _(step):
                    unpack(back, there * quarter + lax.rem(me + step, quarter))

            for shot in range(start, start + size):
                for strip in range(strips):
                    value = stage[strip, shot * rows : (shot + 1) * rows].astype(jnp.bfloat16)
                    traces[group, shot, strip_of(strip), :] = lax.dot_general(
                        value, tables[1], (((0,), (0,)), ((), ())),
                        preferred_element_type=jnp.float32,
                    ).astype(jnp.bfloat16)
            give(group, index).start()

    sent(totals, back_send_sem).wait_send()
    pltpu.make_async_copy(traces, out_ref, out_sem).wait()


def local(records, surface, mirror):
    chips = lax.axis_size("shot")
    cores = lax.axis_size("pair")
    groups, shots, receivers, time = records.shape
    freqs = surface.shape[0]
    parts = 2 * freqs
    tables = jnp.asarray(make_tables(freqs * chips, time))
    tall = chips * shots
    block_shape = (chips, groups, parts, shots, receivers)
    dma = pltpu.SemaphoreType.DMA
    scratch = [
        (records.shape, jnp.bfloat16),
        ((receivers // LANES, shots * chips * parts, LANES), jnp.float32),
        (block_shape, jnp.bfloat16),
        ((cores, groups, parts, chips, shots, receivers), jnp.bfloat16),
        ((tall, 2 * receivers), jnp.bfloat16),
        ((2 * tall, 2 * receivers), jnp.bfloat16),
        ((tall, 2 * receivers), jnp.float32),
        (block_shape, jnp.bfloat16),
        (block_shape, jnp.bfloat16),
    ]
    held_bytes = sum(math.prod(shape) * jnp.dtype(kind).itemsize for shape, kind in scratch)
    roomy = held_bytes < 24 * 1024 * 1024
    grant = held_bytes + 8 * 1024 * 1024 if roomy else VMEM_BYTES
    out_shape = pltpu.VMEM if roomy else jax.ShapeDtypeStruct
    hbm = pl.BlockSpec(memory_space=pltpu.HBM)
    return pl.pallas_call(
        functools.partial(kernel, chips, cores),
        out_shape=out_shape(records.shape, jnp.bfloat16),
        in_specs=[hbm] * 4,
        out_specs=pl.BlockSpec(memory_space=pl.ANY),
        scratch_shapes=[
            *(pltpu.VMEM(shape, kind) for shape, kind in scratch),
            pltpu.VMEM(surface.shape, jnp.float32),
            pltpu.VMEM(tables.shape, tables.dtype),
            pltpu.SMEM(mirror.shape, jnp.int32),
            dma((3,)),
            dma((groups, 2)),
            dma((groups,)),
            dma,
            dma((groups, 4)),
            dma((max(cores - 1, 1), 2)),
            dma,
            dma((groups, 2, 4)),
            dma,
            pltpu.SemaphoreType.REGULAR,
        ],
        compiler_params=pltpu.CompilerParams(
            collective_id=0, has_side_effects=True, vmem_limit_bytes=grant
        ),
    )(
        pltpu.with_memory_space_constraint(mirror, pltpu.HBM),
        pltpu.with_memory_space_constraint(surface, pltpu.HBM),
        pltpu.with_memory_space_constraint(tables, pltpu.HBM),
        pltpu.with_memory_space_constraint(records, pltpu.HBM),
    )


def solution(mesh):
    return jax.shard_map(
        local,
        mesh=mesh,
        in_specs=(P("pair", "shot", None, None), P("shot", None), P()),
        out_specs=P("pair", "shot", None, None),
        check_vma=False,
    )
```

time: 64.4 us -> 60.2 us (0.935)
  matrix products: 3.31 us -> 0 us
  Pallas kernels: 60.4 us -> 57.7 us
  local copies, waits for them, and re-layouts: 0 us -> 2.19 us
    dot_general x1 -> x0, matrix products: 3.31 us -> none  [local(): jnp.einsum('gskr,kt->gsrt', total, inverse, preferred_element_type=jnp.fl...]
    pallas_call x1, Pallas kernels: 60.4 us -> 57.7 us  [local(): pl.pallas_call(functools.partial(kernel, chips, cores), out_shape=out_sha...]
    unnamed x0 -> x1, local copies, waits for them, and re-layouts: none -> 2.19 us
where the time goes in v2:
time: 60.2 us; the launch traced here: 59.9 us
  Pallas kernels  57.7 us (96%)
  local copies, waits for them, and re-layouts  2.19 us (4%)
    pallas_call x1, Pallas kernels, local(): pl.pallas_call(functools.partial(kernel, chips, cores), out_shape=out_sha...  57.7 us
    unnamed x1, local copies, waits for them, and re-layouts  2.19 us

profile of v2, /device:TPU:12, one launch (start us, length us, event | category | flops | bytes accessed | tf_op | source)
XLA Modules:
  0.0 59.9 jit_solution(11536207837725131214)
XLA Ops:
  0.0 57.7 %shard_map.46 = bf16[2,24,384,128]{3,2,1,0:T(8,128)(2,1)S(1)} custom-call(s32[4]{0:T(128)} %mirror_hbm.1, f32[1,384]{1,0:T(1,128)} %surface_hbm.1, bf16[2,32,128]{2,1,0:T(8,128)(2,1)} %constant.2.clone.tables_hbm, bf16[2,24,384,128]{3,2,1,0:T(8,128)(2,1)} %records_ref.1), custom_call_target="tpu_custom_call" | custom-call | tf_op jit(solution)/shard_map/pallas_call | solution.py:364
  57.7 2.2 %copy.6 = bf16[2,24,384,128]{3,2,1,0:T(8,128)(2,1)} copy(bf16[2,24,384,128]{3,2,1,0:T(8,128)(2,1)S(1)} %shard_map.46) | data formatting | bytes 9437184

commit v3 on v2

--- a/solution.py
+++ b/solution.py
@@ -29,16 +29,46 @@
     whole = ((0, shots),)
     if shots % 8 or shots < 16:
         return whole, whole
-    first = ((0, 8), (8, shots - 8)) if group == 0 else whole
+    first = tuple((start, 8) for start in range(0, shots, 8)) if group == 0 else whole
     last = ((0, shots - 8), (shots - 8, 8)) if group + 1 == groups else whole
     return first, last
 
 
+def inverse(value, table):
+    total = lax.dot_general(
+        value.astype(jnp.bfloat16), table, (((0,), (0,)), ((), ())),
+        preferred_element_type=jnp.float32,
+    )
+    return total.astype(jnp.bfloat16)
+
+
+def finish(some_ref, rest, table, out_ref, piece, sems):
+    group, size = some_ref.shape[0] - 1, piece.shape[0]
+    start = some_ref.shape[1] - size
+    rows = rest.shape[1] // size
+    copies = [
+        pltpu.make_async_copy(some_ref.at[:group], out_ref.at[:group], sems.at[0]),
+        pltpu.make_async_copy(
+            some_ref.at[group, pl.ds(0, start)], out_ref.at[group, pl.ds(0, start)], sems.at[1]
+        ),
+        pltpu.make_async_copy(piece, out_ref.at[group, pl.ds(start, size)], sems.at[2]),
+    ]
+    copies[0].start()
+    copies[1].start()
+    for shot in range(size):
+        for strip in range(rest.shape[0]):
+            piece[shot, strip * LANES : (strip + 1) * LANES, :] = inverse(
+                rest[strip, shot * rows : (shot + 1) * rows], table[...]
+            )
+    copies[2].start()
+    for copy in copies:
+        copy.wait()
+
+
 def kernel(
-    chips, cores, mirror_hbm, surface_hbm, tables_hbm, records_ref, out_ref,
-    traces, stage, send, held, left, block, first, totals, back, surface_ref, tables, mirror_ref,
-    small_sems, load_sems, own_sems, send_sem, recv_sems, pass_sems, back_send_sem, back_recv_sems, out_sem,
-    entered,
+    chips, cores, mirror_hbm, surface_hbm, tables_hbm, records_ref, traces, rest, table_out,
+    stage, send, held, left, block, first, totals, back, surface_ref, tables, mirror_ref,
+    small_sems, load_sems, own_sems, send_sem, recv_sems, pass_sems, back_send_sem, back_recv_sems, entered,
 ):
     me = lax.axis_index("shot")
     core = lax.axis_index("pair")
@@ -50,6 +80,7 @@
     quarter = chips // 4
     across = jnp.where(me < half, 0, 1)
     plane = me // quarter
+    place = lax.rem(me, quarter)
     planes = (plane, plane + 1 - 2 * lax.rem(plane, 2), 3 * (1 - across), 2 - across)
     cuts = [cut(shots, group, groups) for group in range(groups)]
 
@@ -60,31 +91,30 @@
         return plane * quarter + lax.rem(me + step, quarter)
 
     def upright(there):
-        return there * quarter + lax.rem(me, quarter)
+        return there * quarter + place
 
     def peer(step):
         return lax.rem(core + step, cores)
 
-    def turned(index, size):
-        inner = lax.rem(index + me, size) + size * (index // size)
-        return lax.rem(across * size + inner, 2 * size)
-
-    def middle(index):
-        return quarter + turned(index, quarter)
-
-    def outer(index):
-        place = turned(index, quarter)
-        return jnp.where(place < quarter, place, place + half)
-
-    def load(group, index):
-        some = pl.ds(*cuts[group][0][index])
+    def flipped(there, flip):
+        spot = place
+        for bit in range(flip.bit_length()):
+            if flip >> bit & 1:
+                spot = spot + (1 << bit) - (2 << bit) * lax.rem(spot // (1 << bit), 2)
+        return there * quarter + spot
+
+    def load(group, some):
         return pltpu.make_async_copy(
-            records_ref.at[group, some], traces.at[group, some], load_sems.at[group, index]
-        )
-
-    for group in range(groups):
-        for index in range(len(cuts[group][0])):
-            load(group, index).start()
+            records_ref.at[group, some], traces.at[group, some], load_sems.at[group, int(some.start > 0)]
+        )
+
+    split = cuts[0][0][0][1]
+    loads = [(0, pl.ds(0, split))]
+    if split < shots:
+        loads.append((0, pl.ds(split, shots - split)))
+    loads.extend((group, pl.ds(0, shots)) for group in range(1, groups))
+    for some in loads[:2]:
+        load(*some).start()
     surface_copy = pltpu.make_async_copy(surface_hbm, surface_ref, small_sems.at[0])
     mirror_copy = pltpu.make_async_copy(mirror_hbm, mirror_ref, small_sems.at[1])
     tables_copy = pltpu.make_async_copy(tables_hbm, tables, small_sems.at[2])
@@ -172,24 +202,25 @@
             device_id_type=MESH,
         )
 
-    def give(group, index):
-        some = pl.ds(*cuts[group][1][index])
-        return pltpu.make_async_copy(
-            traces.at[group, some], out_ref.at[group, some], out_sem
-        )
-
-    def spread_half(target_of, group):
-        @pl.loop(0, half)
-        def _(step):
-            target = target_of(step)
-
-            @pl.when(lax.rem(target, quarter) != lax.rem(me, quarter) if group == 0 else target != me)
-            def _():
-                spread(me, target, group, pl.ds(0, shots)).start()
+    def to_level(there, start, last=0):
+        for flip in range(quarter - 1, last - 1, -1):
+            target = flipped(there, flip)
+            if flip > 0:
+                start(target)
+            else:
+                pl.when(target != me)(functools.partial(start, target))
+
+    def spread_level(there, group):
+        to_level(there, lambda target: spread(me, target, group, pl.ds(0, shots)).start(), int(group == 0))
 
     def spectra(group, index):
         start, size = cuts[group][0][index]
-        load(group, index).wait()
+        for some in loads:
+            if some[0] == group and some[1].start == start:
+                load(*some).wait()
+                if some == loads[0]:
+                    for other in loads[2:]:
+                        load(*other).start()
         for shot in range(start, start + size):
             value = lax.dot_general(
                 tables[0], traces[group, shot], (((1,), (1,)), ((), ())),
@@ -205,7 +236,7 @@
                 )
 
     tables_copy.wait()
-    for index in range(len(cuts[0][0])):
+    for index, piece in enumerate(cuts[0][0]):
         spectra(0, index)
         if index == 0:
             pl.semaphore_wait(barrier, quarter + 2 + cores - 1)
@@ -215,18 +246,21 @@
                 pl.semaphore_signal(entered, inc=1, device_id=(core, level(step)), device_id_type=MESH)
 
         for order in (3, 2, 1):
-            spread(me, upright(planes[order]), 0, pl.ds(*cuts[0][0][index])).start()
+            spread(me, upright(planes[order]), 0, pl.ds(*piece)).start()
     keep(0).start()
     pl.semaphore_wait(entered, quarter - 1)
-    spread_half(middle, 0)
-    for group in range(1, groups):
-        for index in range(len(cuts[group][0])):
-            spectra(group, index)
-        spread_half(middle, group)
-        keep(group).start()
     for group in range(groups):
-        spread_half(outer, group)
-
+        if group > 0:
+            spectra(group, 0)
+            keep(group).start()
+        spread_level(2 - across, group)
+        spread_level(1 + across, group)
+    for group in range(groups):
+        spread_level(3 * (1 - across), group)
+        spread_level(3 * across, group)
+
+    if table_out is not None:
+        table_out[...] = tables[1]
     surface_copy.wait()
     mirror_copy.wait()
     for group in range(groups):
@@ -287,52 +321,56 @@
                         wide = jnp.concatenate([scale, scale], axis=1)
                         left[band, :] = (product * wide).astype(jnp.bfloat16)
 
-        last = group + 1 == groups
+        ahead = (1 - across) * half
         pieces = range(len(cuts[group][1]))
-        if last:
+        if group + 1 == groups:
             for index in pieces:
-                send_back(me, (1 - across) * half, group, index).start()
-        for index in pieces:
-
-            @pl.loop(1 if last else 0, chips)
-            def _(step):
-                target = lax.rem((1 - across) * half + step, chips) if last else turned(step, half)
-
-                @pl.when(target != me)
-                def _():
-                    send_back(me, target, group, index).start()
+                send_back(me, ahead, group, index).start()
+        for beyond in (True, False):
+            for index in pieces:
+
+                def start(target):
+                    send = send_back(me, target, group, index).start
+                    if beyond and group + 1 == groups:
+                        pl.when(target != ahead)(send)
+                    else:
+                        send()
+
+                low = 2 * (1 - across) if beyond else 2 * across
+                to_level(low, start)
+                to_level(low + 1, start)
 
     sent(send, send_sem).wait_send()
 
     for group in range(groups):
         for index, (start, size) in enumerate(cuts[group][1]):
+
+            last = group + 1 == groups and index + 1 == len(cuts[group][1])
+            there, offset = (rest, 0) if last and rest is not None else (stage, start)
 
             def unpack(buffer, source):
                 for part in range(parts):
                     value = buffer[source, group, part, start : start + size].astype(jnp.float32)
-                    place = start * rows + source * parts + part
+                    row = offset * rows + source * parts + part
                     for strip in range(strips):
-                        stage[strip, pl.ds(place, size, stride=rows), :] = value[:, strip_of(strip)]
+                        there[strip, pl.ds(row, size, stride=rows), :] = value[:, strip_of(strip)]
 
             unpack(totals, me)
-            for order, there in enumerate(planes):
-                returned(group, index, there, quarter - 1 if order == 0 else quarter).wait_recv()
-
-                @pl.loop(1 if order == 0 else 0, quarter)
+            for order, away in enumerate(planes):
+                returned(group, index, away, quarter if order else quarter - 1).wait_recv()
+
+                @pl.loop(0 if order else 1, quarter)
                 def _(step):
-                    unpack(back, there * quarter + lax.rem(me + step, quarter))
-
-            for shot in range(start, start + size):
-                for strip in range(strips):
-                    value = stage[strip, shot * rows : (shot + 1) * rows].astype(jnp.bfloat16)
-                    traces[group, shot, strip_of(strip), :] = lax.dot_general(
-                        value, tables[1], (((0,), (0,)), ((), ())),
-                        preferred_element_type=jnp.float32,
-                    ).astype(jnp.bfloat16)
-            give(group, index).start()
+                    unpack(back, away * quarter + lax.rem(me + step, quarter))
+
+            if there is not rest:
+                for shot in range(start, start + size):
+                    for strip in range(strips):
+                        traces[group, shot, strip_of(strip), :] = inverse(
+                            stage[strip, shot * rows : (shot + 1) * rows], tables[1]
+                        )
 
     sent(totals, back_send_sem).wait_send()
-    pltpu.make_async_copy(traces, out_ref, out_sem).wait()
 
 
 def local(records, surface, mirror):
@@ -346,7 +384,6 @@
     block_shape = (chips, groups, parts, shots, receivers)
     dma = pltpu.SemaphoreType.DMA
     scratch = [
-        (records.shape, jnp.bfloat16),
         ((receivers // LANES, shots * chips * parts, LANES), jnp.float32),
         (block_shape, jnp.bfloat16),
         ((cores, groups, parts, chips, shots, receivers), jnp.bfloat16),
@@ -357,15 +394,29 @@
         (block_shape, jnp.bfloat16),
     ]
     held_bytes = sum(math.prod(shape) * jnp.dtype(kind).itemsize for shape, kind in scratch)
-    roomy = held_bytes < 24 * 1024 * 1024
-    grant = held_bytes + 8 * 1024 * 1024 if roomy else VMEM_BYTES
-    out_shape = pltpu.VMEM if roomy else jax.ShapeDtypeStruct
+    out_bytes = records.size * records.dtype.itemsize
+    size = cut(shots, groups - 1, groups)[1][-1][1]
+    roomy = held_bytes + 2 * out_bytes < 32 * 1024 * 1024 and size < shots
+    grant = held_bytes + out_bytes + 8 * 1024 * 1024 if roomy else VMEM_BYTES
     hbm = pl.BlockSpec(memory_space=pltpu.HBM)
-    return pl.pallas_call(
-        functools.partial(kernel, chips, cores),
-        out_shape=out_shape(records.shape, jnp.bfloat16),
+    vmem = pl.BlockSpec(memory_space=pltpu.VMEM)
+    if roomy:
+        rest_shape = (receivers // LANES, size * chips * parts, LANES)
+        body = functools.partial(kernel, chips, cores)
+        out_shape = [pltpu.VMEM(records.shape, jnp.bfloat16), pltpu.VMEM(rest_shape, jnp.float32)]
+        out_shape.append(pltpu.VMEM(tables.shape[1:], tables.dtype))
+        out_specs = [vmem] * 3
+    else:
+        def body(mirror_hbm, surface_hbm, tables_hbm, records_ref, out_ref, *others):
+            kernel(chips, cores, mirror_hbm, surface_hbm, tables_hbm, records_ref, out_ref, None, None, *others)
+
+        out_shape = jax.ShapeDtypeStruct(records.shape, jnp.bfloat16)
+        out_specs = vmem
+    result = pl.pallas_call(
+        body,
+        out_shape=out_shape,
         in_specs=[hbm] * 4,
-        out_specs=pl.BlockSpec(memory_space=pl.ANY),
+        out_specs=out_specs,
         scratch_shapes=[
             *(pltpu.VMEM(shape, kind) for shape, kind in scratch),
             pltpu.VMEM(surface.shape, jnp.float32),
@@ -379,7 +430,6 @@
             dma((max(cores - 1, 1), 2)),
             dma,
             dma((groups, 2, 4)),
-            dma,
             pltpu.SemaphoreType.REGULAR,
         ],
         compiler_params=pltpu.CompilerParams(
@@ -391,6 +441,19 @@
         pltpu.with_memory_space_constraint(tables, pltpu.HBM),
         pltpu.with_memory_space_constraint(records, pltpu.HBM),
     )
+    if not roomy:
+        return result
+    piece = (size, receivers, time)
+    return pl.pallas_call(
+        finish,
+        out_shape=jax.ShapeDtypeStruct(records.shape, jnp.bfloat16),
+        in_specs=[pl.BlockSpec(memory_space=pl.ANY), vmem, vmem],
+        out_specs=hbm,
+        scratch_shapes=[pltpu.VMEM(piece, jnp.bfloat16), dma((3,))],
+        compiler_params=pltpu.CompilerParams(
+            vmem_limit_bytes=2 * math.prod(piece) + 4 * math.prod(rest_shape) + 2 * 1024 * 1024
+        ),
+    )(*result)
 
 
 def solution(mesh):

time: 60.2 us -> 59.3 us (0.985)
  local copies, waits for them, and re-layouts: 2.19 us -> 0 us
  Pallas kernels: 57.7 us -> 58.5 us
    unnamed x1 -> x0, local copies, waits for them, and re-layouts: 2.19 us -> none
    pallas_call x1 -> x2, Pallas kernels: 57.7 us -> 58.5 us  [the longest x1 56.3 us: local(): pl.pallas_call(body, out_shape=out_shape, in_specs=[hbm] * 4, out_specs=o...]
where the time goes in v3:
time: 59.3 us; the launch traced here: 58.5 us
  Pallas kernels  58.5 us (99%)
    pallas_call x1, Pallas kernels, local(): pl.pallas_call(body, out_shape=out_shape, in_specs=[hbm] * 4, out_specs=o...  56.3 us
    pallas_call x1, Pallas kernels, local(): pl.pallas_call(finish, out_shape=jax.ShapeDtypeStruct(records.shape, jnp....  2.2 us

profile of v3, /device:TPU:12, one launch (start us, length us, event | category | flops | bytes accessed | tf_op | source)
XLA Modules:
  0.0 58.5 jit_solution(3456067207650916709)
XLA Ops:
  0.0 56.3 %shard_map.46 = (bf16[2,24,384,128]{3,2,1,0:T(8,128)(2,1)S(1)}, f32[3,256,128]{2,1,0:T(8,128)S(1)}, bf16[32,128]{1,0:T(8,128)(2,1)S(1)}) custom-call(s32[4]{0:T(128)} %mirror_hbm.1, f32[1,384]{1,0:T(1,128)} %surface_hbm.1, bf16[2,32,128]{2,1,0:T(8,128)(2,1)} %constant.2.clone.tables_hbm, bf16[2,24,384,128]{3,2,1,0:T(8,128)(2,1)} %records_ref.1), custom_call_target="tpu_custom_call" | custom-call | tf_op jit(solution)/shard_map/pallas_call | solution.py:415
  56.3 2.2 %shard_map.47 = bf16[2,24,384,128]{3,2,1,0:T(8,128)(2,1)} custom-call(bf16[2,24,384,128]{3,2,1,0:T(8,128)(2,1)S(1)} %get-tuple-element.8.some_ref, f32[3,256,128]{2,1,0:T(8,128)S(1)} %get-tuple-element.9.rest, bf16[32,128]{1,0:T(8,128)(2,1)S(1)} %get-tuple-element.10.table), custom_call_target="tpu_custom_call" | custom-call | tf_op jit(solution)/shard_map/pallas_call | solution.py:447

commit v4 on v3

--- a/solution.py
+++ b/solution.py
@@ -68,7 +68,7 @@
 def kernel(
     chips, cores, mirror_hbm, surface_hbm, tables_hbm, records_ref, traces, rest, table_out,
     stage, send, held, left, block, first, totals, back, surface_ref, tables, mirror_ref,
-    small_sems, load_sems, own_sems, send_sem, recv_sems, pass_sems, back_send_sem, back_recv_sems, entered,
+    small_sems, load_sems, own_sem, send_sem, recv_sems, pass_sems, back_send_sem, back_recv_sems, entered,
 ):
     me = lax.axis_index("shot")
     core = lax.axis_index("pair")
@@ -80,6 +80,7 @@
     quarter = chips // 4
     across = jnp.where(me < half, 0, 1)
     plane = me // quarter
+    middle = lax.rem(plane + 1, 4) // 2
     place = lax.rem(me, quarter)
     planes = (plane, plane + 1 - 2 * lax.rem(plane, 2), 3 * (1 - across), 2 - across)
     cuts = [cut(shots, group, groups) for group in range(groups)]
@@ -105,9 +106,11 @@
 
     def load(group, some):
         return pltpu.make_async_copy(
-            records_ref.at[group, some], traces.at[group, some], load_sems.at[group, int(some.start > 0)]
-        )
-
+            records_ref.at[group, some], traces.at[group, some], load_sems.at[group + int(group + some.start > 0)]
+        )
+
+    tables_copy = pltpu.make_async_copy(tables_hbm, tables, small_sems.at[2])
+    tables_copy.start()
     split = cuts[0][0][0][1]
     loads = [(0, pl.ds(0, split))]
     if split < shots:
@@ -117,8 +120,6 @@
         load(*some).start()
     surface_copy = pltpu.make_async_copy(surface_hbm, surface_ref, small_sems.at[0])
     mirror_copy = pltpu.make_async_copy(mirror_hbm, mirror_ref, small_sems.at[1])
-    tables_copy = pltpu.make_async_copy(tables_hbm, tables, small_sems.at[2])
-    tables_copy.start()
     surface_copy.start()
     mirror_copy.start()
 
@@ -138,18 +139,18 @@
             src_ref=send.at[target, group, :, some],
             dst_ref=held.at[core, group, :, source, some],
             send_sem=send_sem,
-            recv_sem=recv_sems.at[group, source // quarter],
+            recv_sem=recv_sems.at[source // quarter],
             device_id=(core, target),
             device_id_type=MESH,
         )
 
-    def arrived(group, there, count):
-        some = held.at[core, group, :, pl.ds(0, count)]
+    def arrived(there, count):
+        some = held.at[core, :, :, pl.ds(0, count)]
         return pltpu.make_async_remote_copy(
             src_ref=some,
             dst_ref=some,
             send_sem=send_sem,
-            recv_sem=recv_sems.at[group, there],
+            recv_sem=recv_sems.at[there],
             device_id=(core, me),
             device_id_type=MESH,
         )
@@ -164,29 +165,31 @@
             device_id_type=MESH,
         )
 
-    def keep(group):
-        return pltpu.make_async_copy(
-            send.at[me, group], held.at[core, group, :, me], own_sems.at[group]
-        )
+    def keep():
+        return pltpu.make_async_copy(send.at[me], held.at[core, :, :, me], own_sem)
+
+    def batch(group, index, kind):
+        return group + (3 * index + kind if group + 1 == groups else 0)
 
     def send_back(source, target, group, index):
+        kind = jnp.where(target // half == across, 0, 1 + middle)
         some = pl.ds(*cuts[group][1][index])
         return pltpu.make_async_remote_copy(
             src_ref=totals.at[target, group, :, some],
             dst_ref=back.at[source, group, :, some],
             send_sem=back_send_sem,
-            recv_sem=back_recv_sems.at[group, index, source // quarter],
+            recv_sem=back_recv_sems.at[batch(group, index, kind)],
             device_id=(core, target),
             device_id_type=MESH,
         )
 
-    def returned(group, index, there, count):
+    def returned(group, index, kind, count):
         some = back.at[pl.ds(0, count), group, :, pl.ds(*cuts[group][1][index])]
         return pltpu.make_async_remote_copy(
             src_ref=some,
             dst_ref=some,
             send_sem=back_send_sem,
-            recv_sem=back_recv_sems.at[group, index, there],
+            recv_sem=back_recv_sems.at[batch(group, index, kind)],
             device_id=(core, me),
             device_id_type=MESH,
         )
@@ -197,7 +200,7 @@
             src_ref=some,
             dst_ref=some,
             send_sem=sem,
-            recv_sem=recv_sems.at[0, 0],
+            recv_sem=recv_sems.at[0],
             device_id=(core, me),
             device_id_type=MESH,
         )
@@ -247,12 +250,12 @@
 
         for order in (3, 2, 1):
             spread(me, upright(planes[order]), 0, pl.ds(*piece)).start()
-    keep(0).start()
     pl.semaphore_wait(entered, quarter - 1)
     for group in range(groups):
         if group > 0:
             spectra(group, 0)
-            keep(group).start()
+        if group + 1 == groups:
+            keep().start()
         spread_level(2 - across, group)
         spread_level(1 + across, group)
     for group in range(groups):
@@ -263,13 +266,11 @@
         table_out[...] = tables[1]
     surface_copy.wait()
     mirror_copy.wait()
-    for group in range(groups):
-        for order, there in enumerate(planes):
-            if order == 0:
-                keep(group).wait()
-            arrived(group, there, quarter - 1 if order == 0 else quarter).wait_recv()
-            for other in range(1, cores):
-                hand_on(held.at[core, group, :, pl.ds(there * quarter, quarter)], other).start()
+    keep().wait()
+    for order, there in enumerate(planes):
+        arrived(there, quarter if order else quarter - 1).wait_recv()
+        for other in range(1, cores):
+            hand_on(held.at[core, :, :, pl.ds(there * quarter, quarter)], other).start()
     for other in range(1, cores):
         hand_on(held.at[core], other).wait()
 
@@ -324,15 +325,16 @@
         ahead = (1 - across) * half
         pieces = range(len(cuts[group][1]))
         if group + 1 == groups:
-            for index in pieces:
-                send_back(me, ahead, group, index).start()
+            for there in (ahead, ahead + quarter):
+                for index in pieces:
+                    send_back(me, there, group, index).start()
         for beyond in (True, False):
             for index in pieces:
 
                 def start(target):
                     send = send_back(me, target, group, index).start
                     if beyond and group + 1 == groups:
-                        pl.when(target != ahead)(send)
+                        pl.when(lax.rem(target, quarter) != 0)(send)
                     else:
                         send()
 
@@ -356,12 +358,15 @@
                         there[strip, pl.ds(row, size, stride=rows), :] = value[:, strip_of(strip)]
 
             unpack(totals, me)
-            for order, away in enumerate(planes):
-                returned(group, index, away, quarter if order else quarter - 1).wait_recv()
-
-                @pl.loop(0 if order else 1, quarter)
+            spans = [(across * half, half), (3 * (1 - across) * quarter, quarter), ((2 - across) * quarter, quarter)]
+            if group + 1 < groups:
+                spans = [(0, chips)]
+            for kind, (base, count) in enumerate(spans):
+                returned(group, index, kind, count - int(kind == 0)).wait_recv()
+
+                @pl.loop(int(kind == 0), count)
                 def _(step):
-                    unpack(back, away * quarter + lax.rem(me + step, quarter))
+                    unpack(back, base + lax.rem(me + step, count))
 
             if there is not rest:
                 for shot in range(start, start + size):
@@ -423,13 +428,13 @@
             pltpu.VMEM(tables.shape, tables.dtype),
             pltpu.SMEM(mirror.shape, jnp.int32),
             dma((3,)),
-            dma((groups, 2)),
-            dma((groups,)),
+            dma((groups + 1,)),
             dma,
-            dma((groups, 4)),
+            dma,
+            dma((4,)),
             dma((max(cores - 1, 1), 2)),
             dma,
-            dma((groups, 2, 4)),
+            dma((groups + 5,)),
             pltpu.SemaphoreType.REGULAR,
         ],
         compiler_params=pltpu.CompilerParams(

time: 59.3 us -> 59 us (level)
  no operation moved by 1% of the time
where the time goes in v4:
time: 59 us; the launch traced here: 58.3 us
  Pallas kernels  58.3 us (99%)
    pallas_call x1, Pallas kernels, local(): pl.pallas_call(body, out_shape=out_shape, in_specs=[hbm] * 4, out_specs=o...  56.1 us
    pallas_call x1, Pallas kernels, local(): pl.pallas_call(finish, out_shape=jax.ShapeDtypeStruct(records.shape, jnp....  2.2 us

profile of v4, /device:TPU:12, one launch (start us, length us, event | category | flops | bytes accessed | tf_op | source)
XLA Modules:
  0.0 58.3 jit_solution(5527268766930401856)
XLA Ops:
  0.0 56.1 %shard_map.46 = (bf16[2,24,384,128]{3,2,1,0:T(8,128)(2,1)S(1)}, f32[3,256,128]{2,1,0:T(8,128)S(1)}, bf16[32,128]{1,0:T(8,128)(2,1)S(1)}) custom-call(s32[4]{0:T(128)} %mirror_hbm.1, f32[1,384]{1,0:T(1,128)} %surface_hbm.1, bf16[2,32,128]{2,1,0:T(8,128)(2,1)} %constant.2.clone.tables_hbm, bf16[2,24,384,128]{3,2,1,0:T(8,128)(2,1)} %records_ref.1), custom_call_target="tpu_custom_call" | custom-call | tf_op jit(solution)/shard_map/pallas_call | solution.py:420
  56.1 2.2 %shard_map.47 = bf16[2,24,384,128]{3,2,1,0:T(8,128)(2,1)} custom-call(bf16[2,24,384,128]{3,2,1,0:T(8,128)(2,1)S(1)} %get-tuple-element.8.some_ref, f32[3,256,128]{2,1,0:T(8,128)S(1)} %get-tuple-element.9.rest, bf16[32,128]{1,0:T(8,128)(2,1)S(1)} %get-tuple-element.10.table), custom_call_target="tpu_custom_call" | custom-call | tf_op jit(solution)/shard_map/pallas_call | solution.py:452

commit v5 on v4

--- a/solution.py
+++ b/solution.py
@@ -30,7 +30,7 @@
     if shots % 8 or shots < 16:
         return whole, whole
     first = tuple((start, 8) for start in range(0, shots, 8)) if group == 0 else whole
-    last = ((0, shots - 8), (shots - 8, 8)) if group + 1 == groups else whole
+    last = ((0, 8), (8, shots - 8)) if group + 1 == groups else whole
     return first, last
 
 
@@ -322,25 +322,32 @@
                         wide = jnp.concatenate([scale, scale], axis=1)
                         left[band, :] = (product * wide).astype(jnp.bfloat16)
 
-        ahead = (1 - across) * half
+        beyond = (1 - across) * half
         pieces = range(len(cuts[group][1]))
-        if group + 1 == groups:
-            for there in (ahead, ahead + quarter):
-                for index in pieces:
-                    send_back(me, there, group, index).start()
-        for beyond in (True, False):
+
+        def rest_of(index):
+            for step in range(2):
+                to_level(
+                    2 * (1 - across) + step,
+                    lambda target: pl.when(lax.rem(target, quarter) != 0)(
+                        send_back(me, target, group, index).start
+                    ),
+                )
+
+        firsts = [0, quarter]
+        if group + 1 == groups and len(pieces) > 1:
             for index in pieces:
-
-                def start(target):
-                    send = send_back(me, target, group, index).start
-                    if beyond and group + 1 == groups:
-                        pl.when(lax.rem(target, quarter) != 0)(send)
-                    else:
-                        send()
-
-                low = 2 * (1 - across) if beyond else 2 * across
-                to_level(low, start)
-                to_level(low + 1, start)
+                for spot in firsts:
+                    send_back(me, beyond + spot, group, index).start()
+            rest_of(0)
+            rest_of(1)
+        else:
+            for index in pieces:
+                for step in range(2):
+                    to_level(2 * (1 - across) + step, lambda target: send_back(me, target, group, index).start())
+        for index in pieces:
+            for step in range(2):
+                to_level(2 * across + step, lambda target: send_back(me, target, group, index).start())
 
     sent(send, send_sem).wait_send()
 

time: 59 us -> 58.5 us (level)
  no operation moved by 1% of the time
where the time goes in v5:
time: 58.5 us; the launch traced here: 58.3 us
  Pallas kernels  58.3 us (100%)
    pallas_call x1, Pallas kernels, local(): pl.pallas_call(body, out_shape=out_shape, in_specs=[hbm] * 4, out_specs=o...  56.1 us
    pallas_call x1, Pallas kernels, local(): pl.pallas_call(finish, out_shape=jax.ShapeDtypeStruct(records.shape, jnp....  2.21 us

profile of v5, /device:TPU:12, one launch (start us, length us, event | category | flops | bytes accessed | tf_op | source)
XLA Modules:
  0.0 58.3 jit_solution(12699792598235442639)
XLA Ops:
  0.0 56.1 %shard_map.46 = (bf16[2,24,384,128]{3,2,1,0:T(8,128)(2,1)S(1)}, f32[3,512,128]{2,1,0:T(8,128)S(1)}, bf16[32,128]{1,0:T(8,128)(2,1)S(1)}) custom-call(s32[4]{0:T(128)} %mirror_hbm.1, f32[1,384]{1,0:T(1,128)} %surface_hbm.1, bf16[2,32,128]{2,1,0:T(8,128)(2,1)} %constant.2.clone.tables_hbm, bf16[2,24,384,128]{3,2,1,0:T(8,128)(2,1)} %records_ref.1), custom_call_target="tpu_custom_call" | custom-call | tf_op jit(solution)/shard_map/pallas_call | solution.py:427
  56.1 2.2 %shard_map.47 = bf16[2,24,384,128]{3,2,1,0:T(8,128)(2,1)} custom-call(bf16[2,24,384,128]{3,2,1,0:T(8,128)(2,1)S(1)} %get-tuple-element.8.some_ref, f32[3,512,128]{2,1,0:T(8,128)S(1)} %get-tuple-element.9.rest, bf16[32,128]{1,0:T(8,128)(2,1)S(1)} %get-tuple-element.10.table), custom_call_target="tpu_custom_call" | custom-call | tf_op jit(solution)/shard_map/pallas_call | solution.py:459

commit v6 on v5

--- a/solution.py
+++ b/solution.py
@@ -46,21 +46,30 @@
     group, size = some_ref.shape[0] - 1, piece.shape[0]
     start = some_ref.shape[1] - size
     rows = rest.shape[1] // size
-    copies = [
-        pltpu.make_async_copy(some_ref.at[:group], out_ref.at[:group], sems.at[0]),
-        pltpu.make_async_copy(
-            some_ref.at[group, pl.ds(0, start)], out_ref.at[group, pl.ds(0, start)], sems.at[1]
-        ),
-        pltpu.make_async_copy(piece, out_ref.at[group, pl.ds(start, size)], sems.at[2]),
-    ]
-    copies[0].start()
-    copies[1].start()
-    for shot in range(size):
-        for strip in range(rest.shape[0]):
-            piece[shot, strip * LANES : (strip + 1) * LANES, :] = inverse(
-                rest[strip, shot * rows : (shot + 1) * rows], table[...]
+    copies = [pltpu.make_async_copy(some_ref.at[:group], out_ref.at[:group], sems.at[0])]
+    if start > 0:
+        copies.append(
+            pltpu.make_async_copy(
+                some_ref.at[group, pl.ds(0, start)], out_ref.at[group, pl.ds(0, start)], sems.at[1]
             )
-    copies[2].start()
+        )
+    for copy in copies:
+        copy.start()
+    chunk = 8 if size % 8 == 0 else size
+    for low in range(0, size, chunk):
+        for shot in range(low, low + chunk):
+            for strip in range(rest.shape[0]):
+                piece[shot, strip * LANES : (strip + 1) * LANES, :] = inverse(
+                    rest[strip, shot * rows : (shot + 1) * rows], table[...]
+                )
+        copies.append(
+            pltpu.make_async_copy(
+                piece.at[pl.ds(low, chunk)],
+                out_ref.at[group, pl.ds(start + low, chunk)],
+                sems.at[2 + low // chunk],
+            )
+        )
+        copies[-1].start()
     for copy in copies:
         copy.wait()
 
@@ -104,20 +113,24 @@
                 spot = spot + (1 << bit) - (2 << bit) * lax.rem(spot // (1 << bit), 2)
         return there * quarter + spot
 
-    def load(group, some):
-        return pltpu.make_async_copy(
-            records_ref.at[group, some], traces.at[group, some], load_sems.at[group + int(group + some.start > 0)]
-        )
-
-    tables_copy = pltpu.make_async_copy(tables_hbm, tables, small_sems.at[2])
-    tables_copy.start()
     split = cuts[0][0][0][1]
-    loads = [(0, pl.ds(0, split))]
+    bit = 4 if split % 4 == 0 else split
+    loads = [(0, pl.ds(start, bit)) for start in range(0, split, bit)]
+    head = len(loads)
     if split < shots:
         loads.append((0, pl.ds(split, shots - split)))
     loads.extend((group, pl.ds(0, shots)) for group in range(1, groups))
-    for some in loads[:2]:
-        load(*some).start()
+
+    def load(index):
+        group, some = loads[index]
+        return pltpu.make_async_copy(
+            records_ref.at[group, some], traces.at[group, some], load_sems.at[index]
+        )
+
+    tables_copy = pltpu.make_async_copy(tables_hbm, tables, small_sems.at[2])
+    tables_copy.start()
+    for index in range(head + int(split < shots)):
+        load(index).start()
     surface_copy = pltpu.make_async_copy(surface_hbm, surface_ref, small_sems.at[0])
     mirror_copy = pltpu.make_async_copy(mirror_hbm, mirror_ref, small_sems.at[1])
     surface_copy.start()
@@ -218,13 +231,13 @@
 
     def spectra(group, index):
         start, size = cuts[group][0][index]
-        for some in loads:
-            if some[0] == group and some[1].start == start:
-                load(*some).wait()
-                if some == loads[0]:
-                    for other in loads[2:]:
-                        load(*other).start()
         for shot in range(start, start + size):
+            for number, (whose, some) in enumerate(loads):
+                if whose == group and some.start == shot:
+                    load(number).wait()
+                    if number == head - 1:
+                        for other in range(head + int(split < shots), len(loads)):
+                            load(other).start()
             value = lax.dot_general(
                 tables[0], traces[group, shot], (((1,), (1,)), ((), ())),
                 preferred_element_type=jnp.float32,
@@ -435,7 +448,7 @@
             pltpu.VMEM(tables.shape, tables.dtype),
             pltpu.SMEM(mirror.shape, jnp.int32),
             dma((3,)),
-            dma((groups + 1,)),
+            dma((groups + 2,)),
             dma,
             dma,
             dma((4,)),
@@ -461,7 +474,7 @@
         out_shape=jax.ShapeDtypeStruct(records.shape, jnp.bfloat16),
         in_specs=[pl.BlockSpec(memory_space=pl.ANY), vmem, vmem],
         out_specs=hbm,
-        scratch_shapes=[pltpu.VMEM(piece, jnp.bfloat16), dma((3,))],
+        scratch_shapes=[pltpu.VMEM(piece, jnp.bfloat16), dma((2 + max(size // 8, 1),))],
         compiler_params=pltpu.CompilerParams(
             vmem_limit_bytes=2 * math.prod(piece) + 4 * math.prod(rest_shape) + 2 * 1024 * 1024
         ),

time: 58.5 us -> 58.5 us (level)
  no operation moved by 1% of the time
where the time goes in v6:
time: 58.5 us; the launch traced here: 58.3 us
  Pallas kernels  58.3 us (100%)
    pallas_call x1, Pallas kernels, local(): pl.pallas_call(body, out_shape=out_shape, in_specs=[hbm] * 4, out_specs=o...  56 us
    pallas_call x1, Pallas kernels, local(): pl.pallas_call(finish, out_shape=jax.ShapeDtypeStruct(records.shape, jnp....  2.21 us

profile of v6, /device:TPU:12, one launch (start us, length us, event | category | flops | bytes accessed | tf_op | source)
XLA Modules:
  0.0 58.3 jit_solution(5881636033362367522)
XLA Ops:
  0.0 56.0 %shard_map.46 = (bf16[2,24,384,128]{3,2,1,0:T(8,128)(2,1)S(1)}, f32[3,512,128]{2,1,0:T(8,128)S(1)}, bf16[32,128]{1,0:T(8,128)(2,1)S(1)}) custom-call(s32[4]{0:T(128)} %mirror_hbm.1, f32[1,384]{1,0:T(1,128)} %surface_hbm.1, bf16[2,32,128]{2,1,0:T(8,128)(2,1)} %constant.2.clone.tables_hbm, bf16[2,24,384,128]{3,2,1,0:T(8,128)(2,1)} %records_ref.1), custom_call_target="tpu_custom_call" | custom-call | tf_op jit(solution)/shard_map/pallas_call | solution.py:440
  56.1 2.2 %shard_map.47 = bf16[2,24,384,128]{3,2,1,0:T(8,128)(2,1)} custom-call(bf16[2,24,384,128]{3,2,1,0:T(8,128)(2,1)S(1)} %get-tuple-element.8.some_ref, f32[3,512,128]{2,1,0:T(8,128)S(1)} %get-tuple-element.9.rest, bf16[32,128]{1,0:T(8,128)(2,1)S(1)} %get-tuple-element.10.table), custom_call_target="tpu_custom_call" | custom-call | tf_op jit(solution)/shard_map/pallas_call | solution.py:472
